TPU v7x, 32 devices: a whole 2x2x4 slice. The times are simulated.
32 devices in a mesh: comp: 4 (over y, x), samp: 8 (over z, core).
Axes of the slice: x: 2, y: 2, z: 4, core: 2. Of those that a mesh axis runs over, the one named last changes fastest.
Arguments:
- samples: float32 [2048, 32768], P('comp', 'samp'), may hold values from -1.7 to 1.7
- unmixing: float32 [2048, 2048], P('comp', 'samp'), may hold values from -0.37565048 to 0.37565048, as said below
Outputs:
- decorrelated: float32 [2048, 2048], P('comp', 'samp')
Inputs may be any that keep to these rules, and one draw needn't show every extreme that they name: `unmixing`: every entry's magnitude is at most 17 / sqrt(2048).
All inputs are finite; a program needn't handle non-finite values.
Results may differ from a plain program's by a relative error of at most 0.00011.
Values sent between devices are 32-bit elements; how exact they have to be, the bound alone decides.
No kernel may reach another device: no remote copies, remote signals or barrier semaphores. Data moves between devices by JAX's collectives and lax.ppermute only.
A program may use at most 128 MiB of HBM per device.

v0:
```python
import jax
import jax.numpy as jnp
from jax import lax
from jax.sharding import PartitionSpec as P

NS_STEPS = 3
highest = lax.Precision.HIGHEST


def on_device(samples, unmixing):
    rows = lax.all_gather(unmixing, "samp", axis=1, tiled=True)
    whole = lax.all_gather(samples, "comp", axis=0, tiled=True)
    count = whole.shape[1] * lax.axis_size("samp")
    order = rows.shape[1]
    projected = jnp.dot(rows, whole, precision=highest)
    contrast = jnp.tanh(projected)
    slope_part = jnp.sum(1.0 - contrast * contrast, axis=1)
    moment_part = lax.dot_general(contrast, whole, (((1,), (1,)), ((), ())), precision=highest)
    moment_total, slope_total = lax.psum((moment_part, slope_part), "samp")
    updated_rows = moment_total / count - (slope_total / count)[:, None] * rows
    width = unmixing.shape[1]
    updated = lax.dynamic_slice_in_dim(updated_rows, lax.axis_index("samp") * width, width, 1)
    squares = lax.psum(jnp.sum(updated * updated), ("comp", "samp"))
    current = updated / (2.5 * jnp.sqrt(squares / order + 1e-06))
    for step in range(NS_STEPS):
        column_panel = lax.all_gather(current, "comp", axis=0, tiled=True)
        gram_part = lax.dot_general(
            current, column_panel, (((1,), (1,)), ((), ())), precision=highest
        )
        gram = lax.psum(gram_part, "samp")
        current = 1.5 * current - 0.5 * jnp.dot(gram, column_panel, precision=highest)
    return current * jnp.sqrt(jnp.float32(order))


def solution(mesh):
    return jax.shard_map(
        on_device,
        mesh=mesh,
        in_specs=(P("comp", "samp"), P("comp", "samp")),
        out_specs=P("comp", "samp"),
        check_vma=False,
    )
```

profile of v0, /device:TPU:0, one launch (start us, length us, event | category | flops | bytes accessed | tf_op | source)
XLA Modules:
  0.0 1060.8 jit_solution(8556810066995463765)
XLA Ops:
  6.5 0.7 all-gather.6.cloned.1.call-update
  7.3 0.0 all-gather.8.cloned.1.call-start
  7.3 0.7 all-gather.8.cloned.1.call-update
  8.0 0.0 all-reduce.5.cloned.1.call-start
  8.1 50.5 %all-gather.6.cloned.1.call-done = f32[512,2048]{1,0:T(8,128)} async-done(((f32[512,256]{1,0:T(8,128)}), f32[512,2048]{1,0:T(8,128)}) %all-gather.6.cloned.1.call-update) | async-done | bytes 4194320 | tf_op jit(solution)/shard_map/all_gather | solution.py:11
  58.6 297.8 %all-gather.8.cloned.1.call-done = f32[2048,4096]{1,0:T(8,128)} async-done(((f32[512,4096]{1,0:T(8,128)}), f32[2048,4096]{1,0:T(8,128)}) %all-gather.8.cloned.1.call-update) | async-done | bytes 33554448 | tf_op jit(solution)/shard_map/all_gather | solution.py:12
  356.3 59.6 %subtract_reduce_fusion = (f32[512]{0:T(512)S(1)}, f32[512,4096]{1,0:T(8,128)S(1)}) fusion(f32[512,2048]{1,0:T(8,128)} %all-gather.6.cloned.1.call-done, f32[2048,4096]{1,0:T(8,128)} %all-gather.8.cloned.1.call-done), kind=kOutput, calls=%fused_computation | convolution fusion | flops 51545899008 | bytes 46139392 | tf_op jit(solution)/shard_map/dot_general | solution.py:15
  415.9 58.4 %fusion = f32[512,2048]{1,0:T(8,128)} fusion(f32[2048,4096]{1,0:T(8,128)} %all-gather.8.cloned.1.call-done, f32[512,4096]{1,0:T(8,128)S(1)} %get-tuple-element.6), kind=kOutput, calls=%fused_computation.1 | convolution fusion | flops 51539607552 | bytes 46137344 | tf_op jit(solution)/shard_map/dot_general | solution.py:18
  474.3 0.0 all-reduce.5.cloned.1.call-update
  474.3 0.0 all-gather.10.cloned.1.call-start
  474.4 16.7 %psum.43 = f32[512]{0:T(512)S(1)} all-reduce(f32[512]{0:T(512)S(1)} %get-tuple-element.5), channel_id=1, replica_groups=mesh['comp'=4,'samp'=8] {'samp'}, use_global_device_ids=true, to_apply=%region_2.0 | all-reduce | flops 512 | bytes 4096 | tf_op jit(solution)/shard_map/psum | solution.py:19
  491.1 80.0 %all-reduce.5.cloned.1.call-done = f32[512,2048]{1,0:T(8,128)} async-done(((f32[512,2048]{1,0:T(8,128)}), f32[512,2048]{1,0:T(8,128)}) %all-reduce.5.cloned.1.call-update) | async-done | bytes 4194320 | tf_op jit(solution)/shard_map/psum | solution.py:19
  571.1 2.0 multiply_reduce_fusion
  573.1 40.4 %psum.44 = f32[]{:T(128)} all-reduce(f32[]{:T(128)} %multiply_reduce_fusion), channel_id=1, replica_groups=mesh['comp'=4,'samp'=8] {'comp','samp'}, use_global_device_ids=true, to_apply=%region_4.0 | all-reduce | flops 1 | bytes 8 | tf_op jit(solution)/shard_map/psum | solution.py:23
  614.2 2.1 broadcast_divide_fusion
  616.4 0.2 all-reduce.7.cloned.1.call-start
  616.7 35.0 %all-gather.10.cloned.1.call-done = f32[2048,256]{1,0:T(8,128)} async-done(((f32[512,256]{1,0:T(8,128)}), f32[2048,256]{1,0:T(8,128)}) %all-gather.10.cloned.1.call-update) | async-done | bytes 2097168 | tf_op jit(solution)/shard_map/all_gather | solution.py:26
  651.7 7.4 fusion.7
  659.1 0.0 all-gather.12.cloned.1.call-start
  659.2 96.6 %all-reduce.7.cloned.1.call-done = f32[512,2048]{1,0:T(8,128)} async-done(((f32[512,2048]{1,0:T(8,128)}), f32[512,2048]{1,0:T(8,128)}) %all-reduce.7.cloned.1.call-update) | async-done | bytes 4194320 | tf_op jit(solution)/shard_map/psum | solution.py:30
  755.8 6.4 fusion.5
  762.2 0.0 all-reduce.9.cloned.1.call-start
  762.3 35.3 %all-gather.12.cloned.1.call-done = f32[2048,256]{1,0:T(8,128)} async-done(((f32[512,256]{1,0:T(8,128)}), f32[2048,256]{1,0:T(8,128)}) %all-gather.12.cloned.1.call-update) | async-done | bytes 2097168 | tf_op jit(solution)/shard_map/all_gather | solution.py:26
  797.6 7.4 fusion.8
  805.0 0.3 all-gather.14.cloned.1.call-start
  805.3 96.4 %all-reduce.9.cloned.1.call-done = f32[512,2048]{1,0:T(8,128)} async-done(((f32[512,2048]{1,0:T(8,128)}), f32[512,2048]{1,0:T(8,128)}) %all-reduce.9.cloned.1.call-update) | async-done | bytes 4194320 | tf_op jit(solution)/shard_map/psum | solution.py:30
  901.7 6.4 fusion.4
  908.2 0.0 all-reduce.11.cloned.1.call-start
  908.2 35.3 %all-gather.14.cloned.1.call-done = f32[2048,256]{1,0:T(8,128)} async-done(((f32[512,256]{1,0:T(8,128)}), f32[2048,256]{1,0:T(8,128)}) %all-gather.14.cloned.1.call-update) | async-done | bytes 2097168 | tf_op jit(solution)/shard_map/all_gather | solution.py:26
  943.5 7.4 fusion.9
  951.0 96.6 %all-reduce.11.cloned.1.call-done = f32[512,2048]{1,0:T(8,128)} async-done(((f32[512,2048]{1,0:T(8,128)}), f32[512,2048]{1,0:T(8,128)}) %all-reduce.11.cloned.1.call-update) | async-done | bytes 4194320 | tf_op jit(solution)/shard_map/psum | solution.py:30
  1047.6 6.4 fusion.3
  (20 shorter events, 0.1 us)
Async XLA Ops:
  6.5 52.0 %all-gather.6.cloned.1.call-start = ((), (), s32[]{:S(2)}) async-start(), calls=%async_computation | async-start | bytes 4718592 | tf_op jit(solution)/shard_map/all_gather | solution.py:11
  7.3 349.1 %all-gather.8.cloned.1.call-start = ((), (), s32[]{:S(2)}) async-start(), calls=%async_computation.1 | async-start | bytes 41943040 | tf_op jit(solution)/shard_map/all_gather | solution.py:12
  8.0 563.1 %all-reduce.5.cloned.1.call-start = ((), (), s32[]{:S(2)}) async-start(), calls=%async_computation.2 | async-start | bytes 8388608 | tf_op jit(solution)/shard_map/psum | solution.py:19
  474.3 177.4 %all-gather.10.cloned.1.call-start = ((), (), s32[]{:S(2)}) async-start(), calls=%async_computation.3 | async-start | bytes 2621440 | tf_op jit(solution)/shard_map/all_gather | solution.py:26
  616.4 139.4 %copy-start.5 = (f32[512,256]{1,0:T(8,128)S(1)}, f32[512,256]{1,0:T(8,128)}, u32[]{:S(2)}) copy-start(f32[512,256]{1,0:T(8,128)} %broadcast_divide_fusion) | copy-start | bytes 1572868
  616.4 139.3 %all-reduce.7.cloned.1.call-start = ((), (), s32[]{:S(2)}) async-start(), calls=%async_computation.4 | async-start | bytes 8388608 | tf_op jit(solution)/shard_map/psum | solution.py:30
  651.7 104.1 %copy-start.2 = (f32[2048,256]{1,0:T(8,128)S(1)}, f32[2048,256]{1,0:T(8,128)}, u32[]{:S(2)}) copy-start(f32[2048,256]{1,0:T(8,128)} %all-gather.10.cloned.1.call-done) | copy-start | bytes 6291460
  659.1 138.5 %all-gather.12.cloned.1.call-start = ((), (), s32[]{:S(2)}) async-start(), calls=%async_computation.5 | async-start | bytes 2621440 | tf_op jit(solution)/shard_map/all_gather | solution.py:26
  762.2 139.5 %copy-start = (f32[512,256]{1,0:T(8,128)S(1)}, f32[512,256]{1,0:T(8,128)}, u32[]{:S(2)}) copy-start(f32[512,256]{1,0:T(8,128)} %fusion.5) | copy-start | bytes 1572868
  762.2 139.4 %all-reduce.9.cloned.1.call-start = ((), (), s32[]{:S(2)}) async-start(), calls=%async_computation.6 | async-start | bytes 8388608 | tf_op jit(solution)/shard_map/psum | solution.py:30
  797.6 104.1 %copy-start.3 = (f32[2048,256]{1,0:T(8,128)S(1)}, f32[2048,256]{1,0:T(8,128)}, u32[]{:S(2)}) copy-start(f32[2048,256]{1,0:T(8,128)} %all-gather.12.cloned.1.call-done) | copy-start | bytes 6291460
  805.0 138.5 %all-gather.14.cloned.1.call-start = ((), (), s32[]{:S(2)}) async-start(), calls=%async_computation.7 | async-start | bytes 2621440 | tf_op jit(solution)/shard_map/all_gather | solution.py:26
  908.1 139.5 %copy-start.1 = (f32[512,256]{1,0:T(8,128)S(1)}, f32[512,256]{1,0:T(8,128)}, u32[]{:S(2)}) copy-start(f32[512,256]{1,0:T(8,128)} %fusion.4) | copy-start | bytes 1572868
  908.2 139.4 %all-reduce.11.cloned.1.call-start = ((), (), s32[]{:S(2)}) async-start(), calls=%async_computation.8 | async-start | bytes 8388608 | tf_op jit(solution)/shard_map/psum | solution.py:30
  943.5 104.1 %copy-start.4 = (f32[2048,256]{1,0:T(8,128)S(1)}, f32[2048,256]{1,0:T(8,128)}, u32[]{:S(2)}) copy-start(f32[2048,256]{1,0:T(8,128)} %all-gather.14.cloned.1.call-done) | copy-start | bytes 6291460
Sparse Core Ops, SparseCore 0:
  8.9 49.5 all-gather.5
  60.4 295.8 all-gather.7
  474.4 96.6 all-reduce.4
  616.5 35.1 all-gather.9
  659.3 96.4 all-reduce.6
  762.3 35.2 all-gather.11
  805.2 96.4 all-reduce.8
  908.3 35.2 all-gather.13
  951.1 96.4 all-reduce.10
where the time goes:
time: 1070 us; the launch traced here: 1060 us
  waiting for transfers between devices  825 us (77%)
  matrix products  159 us (15%)
  blocking collectives  57.1 us (5%)
  between operations  14.2 us (1%)
    all_gather x1, waiting for transfers between devices, on_device(): whole = lax.all_gather(samples, 'comp', axis=0, tiled=True)  298 us
    psum x3, waiting for transfers between devices, on_device(): gram = lax.psum(gram_part, 'samp')  290 us
    all_gather x3, waiting for transfers between devices, on_device(): column_panel = lax.all_gather(current, 'comp', axis=0, tiled=True)  106 us
    psum x1, waiting for transfers between devices, on_device(): moment_total, slope_total = lax.psum((moment_part, slope_part), 'samp')  80 us
    dot_general x1, matrix products, on_device(): projected = jnp.dot(rows, whole, precision=highest)  59.6 us
    dot_general x1, matrix products, on_device(): lax.dot_general(contrast, whole, (((1,), (1,)), ((), ())), precision=high...  58.4 us
    all_gather x1, waiting for transfers between devices, on_device(): rows = lax.all_gather(unmixing, 'samp', axis=1, tiled=True)  50.5 us
    psum x1, blocking collectives, on_device(): squares = lax.psum(jnp.sum(updated * updated), ('comp', 'samp'))  40.4 us
  transfers between devices with their start and end apart: 9, of which 9 were waited for; matrix products, arithmetic and copies ran while one was open for 0% of the time, Pallas kernels for 0%

commit v1 on v0

--- a/solution.py
+++ b/solution.py
@@ -27,7 +27,9 @@
         gram_part = lax.dot_general(
             current, column_panel, (((1,), (1,)), ((), ())), precision=highest
         )
-        gram = lax.psum(gram_part, "samp")
+        gram = gram_part
+        for hop in (1, 2, 4):
+            gram = gram + lax.ppermute(gram, "samp", [(dev, dev ^ hop) for dev in range(8)])
         current = 1.5 * current - 0.5 * jnp.dot(gram, column_panel, precision=highest)
     return current * jnp.sqrt(jnp.float32(order))
 

time: 1070 us -> 1620 us (1.51)
  waiting for transfers between devices: 825 us -> 1370 us
    ppermute x0 -> x9, waiting for transfers between devices: none -> 835 us  [on_device(): lax.ppermute(gram, 'samp', [(dev, dev ^ hop) for dev in range(8)])]
    psum x3 -> x0, waiting for transfers between devices: 290 us -> none  [on_device(): gram = lax.psum(gram_part, 'samp')]
  transfers between devices with their start and end apart: 9 -> 15, of which waited for: 9 -> 15; matrix products, arithmetic and copies ran while one was open for 0% -> 0% of each run, Pallas kernels for 0% -> 0%
where the time goes in v1:
time: 1620 us; the launch traced here: 1610 us
  waiting for transfers between devices  1370 us (85%)
  matrix products  148 us (9%)
  blocking collectives  57.1 us (4%)
    ppermute x9, waiting for transfers between devices, on_device(): lax.ppermute(gram, 'samp', [(dev, dev ^ hop) for dev in range(8)])  835 us
    all_gather x1, waiting for transfers between devices, on_device(): whole = lax.all_gather(samples, 'comp', axis=0, tiled=True)  298 us
    all_gather x3, waiting for transfers between devices, on_device(): column_panel = lax.all_gather(current, 'comp', axis=0, tiled=True)  105 us
    psum x1, waiting for transfers between devices, on_device(): moment_total, slope_total = lax.psum((moment_part, slope_part), 'samp')  80 us
    dot_general x1, matrix products, on_device(): projected = jnp.dot(rows, whole, precision=highest)  59.6 us
    dot_general x1, matrix products, on_device(): lax.dot_general(contrast, whole, (((1,), (1,)), ((), ())), precision=high...  58.2 us
    all_gather x1, waiting for transfers between devices, on_device(): rows = lax.all_gather(unmixing, 'samp', axis=1, tiled=True)  50.5 us
    psum x1, blocking collectives, on_device(): squares = lax.psum(jnp.sum(updated * updated), ('comp', 'samp'))  40.4 us
  transfers between devices with their start and end apart: 15, of which 15 were waited for; matrix products, arithmetic and copies ran while one was open for 0% of the time, Pallas kernels for 0%

profile of v1, /device:TPU:0, one launch (start us, length us, event | category | flops | bytes accessed | tf_op | source)
XLA Modules:
  0.0 1613.2 jit_solution(12703637321558952436)
XLA Ops:
  8.1 50.5 %all-gather.6.cloned.1.call-done = f32[512,2048]{1,0:T(8,128)} async-done(((f32[512,256]{1,0:T(8,128)}), f32[512,2048]{1,0:T(8,128)}) %all-gather.6.cloned.1.call-update) | async-done | bytes 4194320 | tf_op jit(solution)/shard_map/all_gather | solution.py:11
  58.6 297.8 %all-gather.8.cloned.1.call-done = f32[2048,4096]{1,0:T(8,128)} async-done(((f32[512,4096]{1,0:T(8,128)}), f32[2048,4096]{1,0:T(8,128)}) %all-gather.8.cloned.1.call-update) | async-done | bytes 33554448 | tf_op jit(solution)/shard_map/all_gather | solution.py:12
  356.3 59.6 %subtract_reduce_fusion = (f32[512]{0:T(512)S(1)}, f32[512,4096]{1,0:T(8,128)S(1)}) fusion(f32[512,2048]{1,0:T(8,128)} %all-gather.6.cloned.1.call-done, f32[2048,4096]{1,0:T(8,128)} %all-gather.8.cloned.1.call-done), kind=kOutput, calls=%fused_computation | convolution fusion | flops 51545899008 | bytes 46139392 | tf_op jit(solution)/shard_map/dot_general | solution.py:15
  415.9 58.2 %fusion = f32[512,2048]{1,0:T(8,128)} fusion(f32[2048,4096]{1,0:T(8,128)} %all-gather.8.cloned.1.call-done, f32[512,4096]{1,0:T(8,128)S(1)} %get-tuple-element.6), kind=kOutput, calls=%fused_computation.1 | convolution fusion | flops 51539607552 | bytes 46137344 | tf_op jit(solution)/shard_map/dot_general | solution.py:18
  474.1 16.7 %psum.22 = f32[512]{0:T(512)S(1)} all-reduce(f32[512]{0:T(512)S(1)} %get-tuple-element.5), channel_id=1, replica_groups=mesh['comp'=4,'samp'=8] {'samp'}, use_global_device_ids=true, to_apply=%region_2.0 | all-reduce | flops 512 | bytes 4096 | tf_op jit(solution)/shard_map/psum | solution.py:19
  490.9 80.0 %all-reduce.2.cloned.1.call-done = f32[512,2048]{1,0:T(8,128)} async-done(((f32[512,2048]{1,0:T(8,128)}), f32[512,2048]{1,0:T(8,128)}) %all-reduce.2.cloned.1.call-update) | async-done | bytes 4194320 | tf_op jit(solution)/shard_map/psum | solution.py:19
  570.9 2.0 multiply_reduce_fusion
  572.9 40.4 %psum.23 = f32[]{:T(128)} all-reduce(f32[]{:T(128)} %multiply_reduce_fusion), channel_id=1, replica_groups=mesh['comp'=4,'samp'=8] {'comp','samp'}, use_global_device_ids=true, to_apply=%region_4.0 | all-reduce | flops 1 | bytes 8 | tf_op jit(solution)/shard_map/psum | solution.py:23
  614.0 2.1 broadcast_divide_fusion
  616.5 35.0 %all-gather.10.cloned.1.call-done = f32[2048,256]{1,0:T(8,128)} async-done(((f32[512,256]{1,0:T(8,128)}), f32[2048,256]{1,0:T(8,128)}) %all-gather.10.cloned.1.call-update) | async-done | bytes 2097168 | tf_op jit(solution)/shard_map/all_gather | solution.py:26
  651.5 5.6 fusion.25
  657.2 7.1 collective-permute-done
  665.4 1.6 collective-permute-start.1
  667.0 91.1 %collective-permute-done.1 = f32[512,2048]{1,0:T(8,128)S(1)} collective-permute-done((f32[512,2048]{1,0:T(8,128)S(1)}, f32[512,2048]{1,0:T(8,128)S(1)}, u32[]{:S(2)}, u32[]{:S(2)}) %collective-permute-start.1) | collective-permute-done | bytes 4194336 | tf_op jit(solution)/shard_map/ppermute | solution.py:32
  759.2 2.5 collective-permute-start.2
  761.7 180.1 %collective-permute-done.2 = f32[512,2048]{1,0:T(8,128)S(1)} collective-permute-done((f32[512,2048]{1,0:T(8,128)S(1)}, f32[512,2048]{1,0:T(8,128)S(1)}, u32[]{:S(2)}, u32[]{:S(2)}) %collective-permute-start.2) | collective-permute-done | bytes 4194336 | tf_op jit(solution)/shard_map/ppermute | solution.py:32
  941.8 4.3 fusion.17
  946.6 34.9 %all-gather.12.cloned.1.call-done = f32[2048,256]{1,0:T(8,128)} async-done(((f32[512,256]{1,0:T(8,128)}), f32[2048,256]{1,0:T(8,128)}) %all-gather.12.cloned.1.call-update) | async-done | bytes 2097168 | tf_op jit(solution)/shard_map/all_gather | solution.py:26
  981.4 5.6 fusion.26
  987.1 7.1 collective-permute-done.3
  996.9 91.1 %collective-permute-done.4 = f32[512,2048]{1,0:T(8,128)S(1)} collective-permute-done((f32[512,2048]{1,0:T(8,128)S(1)}, f32[512,2048]{1,0:T(8,128)S(1)}, u32[]{:S(2)}, u32[]{:S(2)}) %collective-permute-start.4) | collective-permute-done | bytes 4194336 | tf_op jit(solution)/shard_map/ppermute | solution.py:32
  1089.2 2.5 collective-permute-start.5
  1091.6 180.1 %collective-permute-done.5 = f32[512,2048]{1,0:T(8,128)S(1)} collective-permute-done((f32[512,2048]{1,0:T(8,128)S(1)}, f32[512,2048]{1,0:T(8,128)S(1)}, u32[]{:S(2)}, u32[]{:S(2)}) %collective-permute-start.5) | collective-permute-done | bytes 4194336 | tf_op jit(solution)/shard_map/ppermute | solution.py:32
  1271.8 4.3 multiply_subtract_fusion
  1276.1 35.3 %all-gather.14.cloned.1.call-done = f32[2048,256]{1,0:T(8,128)} async-done(((f32[512,256]{1,0:T(8,128)}), f32[2048,256]{1,0:T(8,128)}) %all-gather.14.cloned.1.call-update) | async-done | bytes 2097168 | tf_op jit(solution)/shard_map/all_gather | solution.py:26
  1311.4 5.8 fusion.27
  1317.3 7.1 collective-permute-done.6
  1325.5 1.6 collective-permute-start.7
  1327.1 91.1 %collective-permute-done.7 = f32[512,2048]{1,0:T(8,128)S(1)} collective-permute-done((f32[512,2048]{1,0:T(8,128)S(1)}, f32[512,2048]{1,0:T(8,128)S(1)}, u32[]{:S(2)}, u32[]{:S(2)}) %collective-permute-start.7) | collective-permute-done | bytes 4194336 | tf_op jit(solution)/shard_map/ppermute | solution.py:32
  1419.3 2.5 collective-permute-start.8
  1421.8 180.1 %collective-permute-done.8 = f32[512,2048]{1,0:T(8,128)S(1)} collective-permute-done((f32[512,2048]{1,0:T(8,128)S(1)}, f32[512,2048]{1,0:T(8,128)S(1)}, u32[]{:S(2)}, u32[]{:S(2)}) %collective-permute-start.8) | collective-permute-done | bytes 4194336 | tf_op jit(solution)/shard_map/ppermute | solution.py:32
  1601.9 4.3 subtract_multiply_fusion
  (35 shorter events, 10.6 us)
Async XLA Ops:
  6.5 52.0 %all-gather.6.cloned.1.call-start = ((), (), s32[]{:S(2)}) async-start(), calls=%async_computation | async-start | bytes 4718592 | tf_op jit(solution)/shard_map/all_gather | solution.py:11
  7.3 349.1 %all-gather.8.cloned.1.call-start = ((), (), s32[]{:S(2)}) async-start(), calls=%async_computation.1 | async-start | bytes 41943040 | tf_op jit(solution)/shard_map/all_gather | solution.py:12
  8.0 562.9 %all-reduce.2.cloned.1.call-start = ((), (), s32[]{:S(2)}) async-start(), calls=%async_computation.2 | async-start | bytes 8388608 | tf_op jit(solution)/shard_map/psum | solution.py:19
  474.1 177.4 %all-gather.10.cloned.1.call-start = ((), (), s32[]{:S(2)}) async-start(), calls=%async_computation.3 | async-start | bytes 2621440 | tf_op jit(solution)/shard_map/all_gather | solution.py:26
  616.2 365.2 %all-gather.12.cloned.1.call-start = ((), (), s32[]{:S(2)}) async-start(), calls=%async_computation.4 | async-start | bytes 2621440 | tf_op jit(solution)/shard_map/all_gather | solution.py:26
  657.1 7.2 collective-permute-start
  665.4 276.4 %copy-start.2 = (f32[2048,256]{1,0:T(8,128)S(1)}, f32[2048,256]{1,0:T(8,128)}, u32[]{:S(2)}) copy-start(f32[2048,256]{1,0:T(8,128)} %all-gather.10.cloned.1.call-done) | copy-start | bytes 6291460
  665.4 276.4 %copy-start.5 = (f32[512,256]{1,0:T(8,128)S(1)}, f32[512,256]{1,0:T(8,128)}, u32[]{:S(2)}) copy-start(f32[512,256]{1,0:T(8,128)} %broadcast_divide_fusion) | copy-start | bytes 1572868
  665.4 92.7 %collective-permute-start.1 = (f32[512,2048]{1,0:T(8,128)S(1)}, f32[512,2048]{1,0:T(8,128)S(1)}, u32[]{:S(2)}, u32[]{:S(2)}) collective-permute-start(f32[512,2048]{1,0:T(8,128)S(1)} %add.41), channel_id=1, source_target_pairs={{0,2},{1,3},{2,0},{3,1},{4,6},{5,7},{6,4},{7,5},{8,10},{9,11},{10,... | collective-permute-start | bytes 12582920 | tf_op jit(solution)/shard_map/ppermute | solution.py:32
  759.2 182.6 %collective-permute-start.2 = (f32[512,2048]{1,0:T(8,128)S(1)}, f32[512,2048]{1,0:T(8,128)S(1)}, u32[]{:S(2)}, u32[]{:S(2)}) collective-permute-start(f32[512,2048]{1,0:T(8,128)S(1)} %add.42), channel_id=1, source_target_pairs={{0,4},{1,5},{2,6},{3,7},{4,0},{5,1},{6,2},{7,3},{8,12},{9,13},{10,... | collective-permute-start | bytes 12582920 | tf_op jit(solution)/shard_map/ppermute | solution.py:32
  946.1 365.3 %all-gather.14.cloned.1.call-start = ((), (), s32[]{:S(2)}) async-start(), calls=%async_computation.5 | async-start | bytes 2621440 | tf_op jit(solution)/shard_map/all_gather | solution.py:26
  987.1 7.2 collective-permute-start.3
  995.4 276.4 %copy-start = (f32[512,256]{1,0:T(8,128)S(1)}, f32[512,256]{1,0:T(8,128)}, u32[]{:S(2)}) copy-start(f32[512,256]{1,0:T(8,128)} %fusion.17) | copy-start | bytes 1572868
  995.4 276.4 %copy-start.3 = (f32[2048,256]{1,0:T(8,128)S(1)}, f32[2048,256]{1,0:T(8,128)}, u32[]{:S(2)}) copy-start(f32[2048,256]{1,0:T(8,128)} %all-gather.12.cloned.1.call-done) | copy-start | bytes 6291460
  995.4 92.7 %collective-permute-start.4 = (f32[512,2048]{1,0:T(8,128)S(1)}, f32[512,2048]{1,0:T(8,128)S(1)}, u32[]{:S(2)}, u32[]{:S(2)}) collective-permute-start(f32[512,2048]{1,0:T(8,128)S(1)} %add.44), channel_id=1, source_target_pairs={{0,2},{1,3},{2,0},{3,1},{4,6},{5,7},{6,4},{7,5},{8,10},{9,11},{10,... | collective-permute-start | bytes 12582920 | tf_op jit(solution)/shard_map/ppermute | solution.py:32
  1089.2 182.6 %collective-permute-start.5 = (f32[512,2048]{1,0:T(8,128)S(1)}, f32[512,2048]{1,0:T(8,128)S(1)}, u32[]{:S(2)}, u32[]{:S(2)}) collective-permute-start(f32[512,2048]{1,0:T(8,128)S(1)} %add.45), channel_id=1, source_target_pairs={{0,4},{1,5},{2,6},{3,7},{4,0},{5,1},{6,2},{7,3},{8,12},{9,13},{10,... | collective-permute-start | bytes 12582920 | tf_op jit(solution)/shard_map/ppermute | solution.py:32
  1317.2 7.2 collective-permute-start.6
  1325.5 276.4 %copy-start.1 = (f32[512,256]{1,0:T(8,128)S(1)}, f32[512,256]{1,0:T(8,128)}, u32[]{:S(2)}) copy-start(f32[512,256]{1,0:T(8,128)} %multiply_subtract_fusion) | copy-start | bytes 1572868
  1325.5 276.4 %copy-start.4 = (f32[2048,256]{1,0:T(8,128)S(1)}, f32[2048,256]{1,0:T(8,128)}, u32[]{:S(2)}) copy-start(f32[2048,256]{1,0:T(8,128)} %all-gather.14.cloned.1.call-done) | copy-start | bytes 6291460
  1325.5 92.7 %collective-permute-start.7 = (f32[512,2048]{1,0:T(8,128)S(1)}, f32[512,2048]{1,0:T(8,128)S(1)}, u32[]{:S(2)}, u32[]{:S(2)}) collective-permute-start(f32[512,2048]{1,0:T(8,128)S(1)} %add.47), channel_id=1, source_target_pairs={{0,2},{1,3},{2,0},{3,1},{4,6},{5,7},{6,4},{7,5},{8,10},{9,11},{10,... | collective-permute-start | bytes 12582920 | tf_op jit(solution)/shard_map/ppermute | solution.py:32
  1419.3 182.6 %collective-permute-start.8 = (f32[512,2048]{1,0:T(8,128)S(1)}, f32[512,2048]{1,0:T(8,128)S(1)}, u32[]{:S(2)}, u32[]{:S(2)}) collective-permute-start(f32[512,2048]{1,0:T(8,128)S(1)} %add.48), channel_id=1, source_target_pairs={{0,4},{1,5},{2,6},{3,7},{4,0},{5,1},{6,2},{7,3},{8,12},{9,13},{10,... | collective-permute-start | bytes 12582920 | tf_op jit(solution)/shard_map/ppermute | solution.py:32
Sparse Core Ops, SparseCore 0:
  8.9 49.5 all-gather.5
  60.4 295.8 all-gather.7
  474.2 96.6 all-reduce.1
  616.3 35.1 all-gather.9
  946.2 35.1 all-gather.11
  1276.2 35.1 all-gather.13
